TPU v7x, 128 devices: a whole 4x4x4 slice. The times are simulated.
128 devices in a mesh: ctx: 16 (over y_hi, z, core), head: 8 (over x, y_lo).
Axes of the slice: x: 4, y: 4 (y_hi: 2, y_lo: 2; y = y_hi * 2 + y_lo), z: 4, core: 2. Of those that a mesh axis runs over, the one named last changes fastest.
Arguments:
- queries: bfloat16 [4096, 8192], P('ctx', 'head'), may hold values from -40 to 40
- keys: bfloat16 [4096, 1024], P('ctx', 'head'), may hold values from -4 to 4
- values: bfloat16 [4096, 1024], P('ctx', 'head'), may hold values from -6 to 6
- out_weight: bfloat16 [8192, 8192], P(None, 'head'), may hold values from -0.1796875 to 0.1796875
- doc_lengths: int32 [16], replicated, may hold values from 1 to 1024, 4096 in all
- owners: int32 [128, 1], replicated, may hold values from 0 to 15; in each aligned block of 8 rows (0 to 7, 8 to 15, ...) no two rows name the same one
Outputs:
- attended: bfloat16 [8192, 8192], P('head', 'ctx')
Inputs may be any that keep to these rules, and one draw needn't show every extreme that they name: `owners`: among the 8 pieces loaded by one index of ctx (aligned blocks of 8 rows) every owner appears at most once. `doc_lengths`: the lengths sum to 4096; the longest is exactly 1024.
All inputs are finite; a program needn't handle non-finite values.
Results may differ from a plain program's by a relative error of at most 0.018.
Values may be sent and summed in bfloat16 or wider, within the bound.
A program may use at most 128 MiB of HBM per device.

v0:
```python
import math
import jax
import jax.numpy as jnp
from jax import lax
from jax.sharding import PartitionSpec as P

HEAD_SIZE = 128
PIECES = 8
MASKED = -1e30


def document_index(positions, doc_starts):
    return jnp.sum((positions[:, None] >= doc_starts[None, :]).astype(jnp.int32), axis=1) - 1


def attend(query_rows, query_pos, keys, values, doc_starts):
    row_count = query_rows.shape[0]
    key_heads = keys.shape[1] // HEAD_SIZE
    group_length = query_rows.shape[1] // keys.shape[1]
    query_heads = query_rows.reshape(row_count, key_heads, group_length, HEAD_SIZE)
    query_doc = document_index(query_pos, doc_starts)
    score_scale = 1.0 / math.sqrt(HEAD_SIZE)
    initial = (
        jnp.full((row_count, key_heads, group_length), MASKED, jnp.float32),
        jnp.zeros((row_count, key_heads, group_length), jnp.float32),
        jnp.zeros((row_count, key_heads, group_length, HEAD_SIZE), jnp.float32),
    )
    key_piece = lax.all_gather(keys, "ctx", axis=0, tiled=True)
    value_piece = lax.all_gather(values, "ctx", axis=0, tiled=True)
    piece_rows = key_piece.shape[0]
    tile_rows = math.gcd(piece_rows, 512)

    def one_tile(tile_index, running):
        tile_start = tile_index * tile_rows
        key_block = lax.dynamic_slice_in_dim(key_piece, tile_start, tile_rows, 0).reshape(
            tile_rows, key_heads, HEAD_SIZE
        )
        value_block = lax.dynamic_slice_in_dim(value_piece, tile_start, tile_rows, 0).reshape(
            tile_rows, key_heads, HEAD_SIZE
        )
        key_pos = tile_start + jnp.arange(tile_rows, dtype=jnp.int32)
        key_doc = document_index(key_pos, doc_starts)
        allowed = (query_doc[:, None] == key_doc[None, :]) & (
            key_pos[None, :] <= query_pos[:, None]
        )
        running_max, running_sum, weighted = running
        scores = (
            jnp.einsum("rkgd,nkd->rkgn", query_heads, key_block, preferred_element_type=jnp.float32)
            * score_scale
        )
        allowed_all = allowed[:, None, None, :]
        scores = jnp.where(allowed_all, scores, MASKED)
        new_max = jnp.maximum(running_max, jnp.max(scores, axis=-1))
        factor = jnp.exp(running_max - new_max)
        weights = jnp.where(allowed_all, jnp.exp(scores - new_max[..., None]), 0.0)
        new_sum = running_sum * factor + jnp.sum(weights, axis=-1)
        new_weighted = weighted * factor[..., None] + jnp.einsum(
            "rkgn,nkd->rkgd",
            weights.astype(jnp.bfloat16),
            value_block,
            preferred_element_type=jnp.float32,
        )
        return (new_max, new_sum, new_weighted)

    final_max, final_sum, weighted = lax.fori_loop(0, piece_rows // tile_rows, one_tile, initial)
    result = weighted / jnp.maximum(final_sum, 1.0)[..., None]
    return result.reshape(row_count, key_heads * group_length * HEAD_SIZE).astype(jnp.bfloat16)


def project(context, out_weight):
    return lax.psum_scatter(
        lax.dot_general(
            out_weight, context, (((1,), (1,)), ((), ())), preferred_element_type=jnp.float32
        ).astype(jnp.bfloat16),
        "head",
        scatter_dimension=0,
        tiled=True,
    )


def per_device(queries, keys, values, out_weight, doc_lengths, owners):
    place_count = lax.axis_size("ctx")
    own_index = lax.axis_index("ctx")
    token_count = queries.shape[0]
    block_rows = token_count // PIECES
    doc_ends = jnp.cumsum(doc_lengths)
    doc_starts = doc_ends - doc_lengths
    owner_table = owners[:, 0].reshape(place_count, PIECES)
    own_owners = lax.dynamic_index_in_dim(owner_table, own_index, 0, keepdims=False)
    place_ids = jnp.arange(place_count, dtype=jnp.int32)
    send_pick = (own_owners[None, :] == place_ids[:, None]).astype(jnp.bfloat16)
    grouped = queries.reshape(PIECES, block_rows, queries.shape[1])
    outgoing = jnp.einsum(
        "oc,chw->ohw", send_pick, grouped, preferred_element_type=jnp.float32
    ).astype(jnp.bfloat16)
    arrived = lax.all_to_all(outgoing, "ctx", split_axis=0, concat_axis=0, tiled=True)
    slot_hits = (owner_table == own_index).astype(jnp.int32)
    slot_live = jnp.sum(slot_hits, axis=1)
    picked = jnp.sum(slot_hits * jnp.arange(PIECES, dtype=jnp.int32)[None, :], axis=1)
    slot_pos = (place_ids[:, None] * PIECES + picked[:, None]) * block_rows + jnp.arange(
        block_rows, dtype=jnp.int32
    )[None, :]
    query_pos = jnp.where(slot_live[:, None] > 0, slot_pos, -1).reshape(-1)
    context = attend(
        arrived.reshape(place_count * block_rows, queries.shape[1]),
        query_pos,
        keys,
        values,
        doc_starts,
    )
    return project(context, out_weight)


def solution(mesh):
    in_specs = (P("ctx", "head"), P("ctx", "head"), P("ctx", "head"), P(None, "head"), P(), P())
    out_specs = P("head", "ctx")
    return jax.shard_map(
        per_device, mesh=mesh, in_specs=in_specs, out_specs=out_specs, check_vma=False
    )
```

profile of v0, /device:TPU:1, one launch (start us, length us, event | category | flops | bytes accessed | tf_op | source)
XLA Modules:
  0.0 447.8 jit_solution(8140803811860141464)
XLA Ops:
  13.0 9.5 %all-to-all-start = ((bf16[16,32,1024]{2,1,0:T(8,128)(2,1)}), bf16[16,32,1024]{2,1,0:T(8,128)(2,1)S(1)}, u32[]{:S(2)}, u32[]{:S(2)}) async-start(bf16[16,32,1024]{2,1,0:T(8,128)(2,1)} %copy.29), calls=%async_computation | async-start | bytes 2097152 | tf_op jit(solution)/shard_map/all_to_all | solution.py:96
  24.5 15.9 %all-to-all-done = bf16[16,32,1024]{2,1,0:T(8,128)(2,1)S(1)} async-done(((bf16[16,32,1024]{2,1,0:T(8,128)(2,1)}), bf16[16,32,1024]{2,1,0:T(8,128)(2,1)S(1)}, u32[]{:S(2)}, u32[]{:S(2)}) %all-to-all-start) | async-done | bytes 1048608 | tf_op jit(solution)/shard_map/all_to_all | solution.py:96
  40.8 20.1 %all-gather.5.cloned.1.call-done = bf16[4096,128]{0,1:T(8,128)(2,1)} async-done(((bf16[256,128]{0,1:T(8,128)(2,1)}), bf16[4096,128]{0,1:T(8,128)(2,1)}) %all-gather.5.cloned.1.call-update) | async-done | bytes 1048592 | tf_op jit(solution)/shard_map/all_gather | solution.py:29
  60.9 47.4 %all-gather.3.cloned.1.call-done = bf16[4096,128]{1,0:T(8,128)(2,1)} async-done(((bf16[256,128]{1,0:T(8,128)(2,1)}), bf16[4096,128]{1,0:T(8,128)(2,1)}) %all-gather.3.cloned.1.call-update) | async-done | bytes 1048592 | tf_op jit(solution)/shard_map/all_gather | solution.py:28
  108.2 131.5 %while.20 = (s32[]{:T(128)}, f32[512,1,8]{0,2,1:T(8,128)S(1)}, f32[512,1,8]{0,2,1:T(8,128)S(1)}, f32[512,1,8,128]{0,3,2,1:T(8,128)}, s32[512]{0:T(512)S(1)}, /*i...) while((s32[]{:T(128)}, f32[512,1,8]{0,2,1:T(8,128)S(1)}, ...), condition=%wide.region_8.9_spmd.clone, body=%wide.region_4.8_spmd.clone.sunk | while | flops 1103414784 | bytes 65560956 | solution.py:65
  108.8 5.6 %fusion.37 = (f32[512,8]{0,1:T(8,128)S(1)}, f32[512,512,8]{1,0,2:T(8,128)}) fusion(pred[512,512]{0,1:T(8,128)(4,1)S(1)} %compare_and_fusion.2, bf16[512,1,8,128]{3,0,2,1:T(8,128)(2,1)S(1)} %get-tuple-element.463, bf16[4096,128]{1,0:T(8,128)(2,1)} %get-tuple-element.462, s32[]{:T(128)S(6)} %select_n.96), kind=kOutput, calls=%fused_computation.3.clone.1 | convolution fusion | flops 543158272 | bytes 9846788 | tf_op jit(solution)/shard_map/while/body/eval_jaxpr/rkgd,nkd->rkgn/dot_general | solution.py:48
  114.4 7.6 %bitcast_add_fusion.5 = f32[512,1,8,128]{0,3,2,1:T(8,128)} fusion(f32[512,1,8,128]{0,3,2,1:T(8,128)} %get-tuple-element.444, f32[512,512,8]{1,0,2:T(8,128)} %get-tuple-element.424, f32[512,8]{0,1:T(8,128)S(1)} %bitcast.90, pred[512,512]{0,1:T(8,128)(4,1)S(1)} %compare_and_fusion.2, f32[512,8]{0,1:T(8,128)S(1)} %get-tuple-element.425, ...), kind=kOutput, calls=%fused_computation.9.clone.1 | convolution fusion | flops 548929536 | bytes 13008901 | tf_op jit(solution)/shard_map/while/body/eval_jaxpr/rkgn,nkd->rkgd/dot_general | solution.py:57
  124.7 5.6 %fusion.37 = (f32[512,8]{0,1:T(8,128)S(1)}, f32[512,512,8]{1,0,2:T(8,128)}) fusion(pred[512,512]{0,1:T(8,128)(4,1)S(1)} %compare_and_fusion.2, bf16[512,1,8,128]{3,0,2,1:T(8,128)(2,1)S(1)} %get-tuple-element.463, bf16[4096,128]{1,0:T(8,128)(2,1)} %get-tuple-element.462, s32[]{:T(128)S(6)} %select_n.96), kind=kOutput, calls=%fused_computation.3.clone.1 | convolution fusion | flops 543158272 | bytes 9846788 | tf_op jit(solution)/shard_map/while/body/eval_jaxpr/rkgd,nkd->rkgn/dot_general | solution.py:48
  130.3 8.2 %bitcast_add_fusion.5 = f32[512,1,8,128]{0,3,2,1:T(8,128)} fusion(f32[512,1,8,128]{0,3,2,1:T(8,128)} %get-tuple-element.444, f32[512,512,8]{1,0,2:T(8,128)} %get-tuple-element.424, f32[512,8]{0,1:T(8,128)S(1)} %bitcast.90, pred[512,512]{0,1:T(8,128)(4,1)S(1)} %compare_and_fusion.2, f32[512,8]{0,1:T(8,128)S(1)} %get-tuple-element.425, ...), kind=kOutput, calls=%fused_computation.9.clone.1 | convolution fusion | flops 548929536 | bytes 13008901 | tf_op jit(solution)/shard_map/while/body/eval_jaxpr/rkgn,nkd->rkgd/dot_general | solution.py:57
  141.2 5.6 %fusion.37 = (f32[512,8]{0,1:T(8,128)S(1)}, f32[512,512,8]{1,0,2:T(8,128)}) fusion(pred[512,512]{0,1:T(8,128)(4,1)S(1)} %compare_and_fusion.2, bf16[512,1,8,128]{3,0,2,1:T(8,128)(2,1)S(1)} %get-tuple-element.463, bf16[4096,128]{1,0:T(8,128)(2,1)} %get-tuple-element.462, s32[]{:T(128)S(6)} %select_n.96), kind=kOutput, calls=%fused_computation.3.clone.1 | convolution fusion | flops 543158272 | bytes 9846788 | tf_op jit(solution)/shard_map/while/body/eval_jaxpr/rkgd,nkd->rkgn/dot_general | solution.py:48
  146.8 8.2 %bitcast_add_fusion.5 = f32[512,1,8,128]{0,3,2,1:T(8,128)} fusion(f32[512,1,8,128]{0,3,2,1:T(8,128)} %get-tuple-element.444, f32[512,512,8]{1,0,2:T(8,128)} %get-tuple-element.424, f32[512,8]{0,1:T(8,128)S(1)} %bitcast.90, pred[512,512]{0,1:T(8,128)(4,1)S(1)} %compare_and_fusion.2, f32[512,8]{0,1:T(8,128)S(1)} %get-tuple-element.425, ...), kind=kOutput, calls=%fused_computation.9.clone.1 | convolution fusion | flops 548929536 | bytes 13008901 | tf_op jit(solution)/shard_map/while/body/eval_jaxpr/rkgn,nkd->rkgd/dot_general | solution.py:57
  157.7 5.6 %fusion.37 = (f32[512,8]{0,1:T(8,128)S(1)}, f32[512,512,8]{1,0,2:T(8,128)}) fusion(pred[512,512]{0,1:T(8,128)(4,1)S(1)} %compare_and_fusion.2, bf16[512,1,8,128]{3,0,2,1:T(8,128)(2,1)S(1)} %get-tuple-element.463, bf16[4096,128]{1,0:T(8,128)(2,1)} %get-tuple-element.462, s32[]{:T(128)S(6)} %select_n.96), kind=kOutput, calls=%fused_computation.3.clone.1 | convolution fusion | flops 543158272 | bytes 9846788 | tf_op jit(solution)/shard_map/while/body/eval_jaxpr/rkgd,nkd->rkgn/dot_general | solution.py:48
  163.3 8.2 %bitcast_add_fusion.5 = f32[512,1,8,128]{0,3,2,1:T(8,128)} fusion(f32[512,1,8,128]{0,3,2,1:T(8,128)} %get-tuple-element.444, f32[512,512,8]{1,0,2:T(8,128)} %get-tuple-element.424, f32[512,8]{0,1:T(8,128)S(1)} %bitcast.90, pred[512,512]{0,1:T(8,128)(4,1)S(1)} %compare_and_fusion.2, f32[512,8]{0,1:T(8,128)S(1)} %get-tuple-element.425, ...), kind=kOutput, calls=%fused_computation.9.clone.1 | convolution fusion | flops 548929536 | bytes 13008901 | tf_op jit(solution)/shard_map/while/body/eval_jaxpr/rkgn,nkd->rkgd/dot_general | solution.py:57
  174.2 5.6 %fusion.37 = (f32[512,8]{0,1:T(8,128)S(1)}, f32[512,512,8]{1,0,2:T(8,128)}) fusion(pred[512,512]{0,1:T(8,128)(4,1)S(1)} %compare_and_fusion.2, bf16[512,1,8,128]{3,0,2,1:T(8,128)(2,1)S(1)} %get-tuple-element.463, bf16[4096,128]{1,0:T(8,128)(2,1)} %get-tuple-element.462, s32[]{:T(128)S(6)} %select_n.96), kind=kOutput, calls=%fused_computation.3.clone.1 | convolution fusion | flops 543158272 | bytes 9846788 | tf_op jit(solution)/shard_map/while/body/eval_jaxpr/rkgd,nkd->rkgn/dot_general | solution.py:48
  179.9 8.2 %bitcast_add_fusion.5 = f32[512,1,8,128]{0,3,2,1:T(8,128)} fusion(f32[512,1,8,128]{0,3,2,1:T(8,128)} %get-tuple-element.444, f32[512,512,8]{1,0,2:T(8,128)} %get-tuple-element.424, f32[512,8]{0,1:T(8,128)S(1)} %bitcast.90, pred[512,512]{0,1:T(8,128)(4,1)S(1)} %compare_and_fusion.2, f32[512,8]{0,1:T(8,128)S(1)} %get-tuple-element.425, ...), kind=kOutput, calls=%fused_computation.9.clone.1 | convolution fusion | flops 548929536 | bytes 13008901 | tf_op jit(solution)/shard_map/while/body/eval_jaxpr/rkgn,nkd->rkgd/dot_general | solution.py:57
  190.7 5.6 %fusion.37 = (f32[512,8]{0,1:T(8,128)S(1)}, f32[512,512,8]{1,0,2:T(8,128)}) fusion(pred[512,512]{0,1:T(8,128)(4,1)S(1)} %compare_and_fusion.2, bf16[512,1,8,128]{3,0,2,1:T(8,128)(2,1)S(1)} %get-tuple-element.463, bf16[4096,128]{1,0:T(8,128)(2,1)} %get-tuple-element.462, s32[]{:T(128)S(6)} %select_n.96), kind=kOutput, calls=%fused_computation.3.clone.1 | convolution fusion | flops 543158272 | bytes 9846788 | tf_op jit(solution)/shard_map/while/body/eval_jaxpr/rkgd,nkd->rkgn/dot_general | solution.py:48
  196.4 8.2 %bitcast_add_fusion.5 = f32[512,1,8,128]{0,3,2,1:T(8,128)} fusion(f32[512,1,8,128]{0,3,2,1:T(8,128)} %get-tuple-element.444, f32[512,512,8]{1,0,2:T(8,128)} %get-tuple-element.424, f32[512,8]{0,1:T(8,128)S(1)} %bitcast.90, pred[512,512]{0,1:T(8,128)(4,1)S(1)} %compare_and_fusion.2, f32[512,8]{0,1:T(8,128)S(1)} %get-tuple-element.425, ...), kind=kOutput, calls=%fused_computation.9.clone.1 | convolution fusion | flops 548929536 | bytes 13008901 | tf_op jit(solution)/shard_map/while/body/eval_jaxpr/rkgn,nkd->rkgd/dot_general | solution.py:57
  207.2 5.6 %fusion.37 = (f32[512,8]{0,1:T(8,128)S(1)}, f32[512,512,8]{1,0,2:T(8,128)}) fusion(pred[512,512]{0,1:T(8,128)(4,1)S(1)} %compare_and_fusion.2, bf16[512,1,8,128]{3,0,2,1:T(8,128)(2,1)S(1)} %get-tuple-element.463, bf16[4096,128]{1,0:T(8,128)(2,1)} %get-tuple-element.462, s32[]{:T(128)S(6)} %select_n.96), kind=kOutput, calls=%fused_computation.3.clone.1 | convolution fusion | flops 543158272 | bytes 9846788 | tf_op jit(solution)/shard_map/while/body/eval_jaxpr/rkgd,nkd->rkgn/dot_general | solution.py:48
  212.9 8.2 %bitcast_add_fusion.5 = f32[512,1,8,128]{0,3,2,1:T(8,128)} fusion(f32[512,1,8,128]{0,3,2,1:T(8,128)} %get-tuple-element.444, f32[512,512,8]{1,0,2:T(8,128)} %get-tuple-element.424, f32[512,8]{0,1:T(8,128)S(1)} %bitcast.90, pred[512,512]{0,1:T(8,128)(4,1)S(1)} %compare_and_fusion.2, f32[512,8]{0,1:T(8,128)S(1)} %get-tuple-element.425, ...), kind=kOutput, calls=%fused_computation.9.clone.1 | convolution fusion | flops 548929536 | bytes 13008901 | tf_op jit(solution)/shard_map/while/body/eval_jaxpr/rkgn,nkd->rkgd/dot_general | solution.py:57
  223.8 5.6 %fusion.37 = (f32[512,8]{0,1:T(8,128)S(1)}, f32[512,512,8]{1,0,2:T(8,128)}) fusion(pred[512,512]{0,1:T(8,128)(4,1)S(1)} %compare_and_fusion.2, bf16[512,1,8,128]{3,0,2,1:T(8,128)(2,1)S(1)} %get-tuple-element.463, bf16[4096,128]{1,0:T(8,128)(2,1)} %get-tuple-element.462, s32[]{:T(128)S(6)} %select_n.96), kind=kOutput, calls=%fused_computation.3.clone.1 | convolution fusion | flops 543158272 | bytes 9846788 | tf_op jit(solution)/shard_map/while/body/eval_jaxpr/rkgd,nkd->rkgn/dot_general | solution.py:48
  229.4 8.2 %bitcast_add_fusion.5 = f32[512,1,8,128]{0,3,2,1:T(8,128)} fusion(f32[512,1,8,128]{0,3,2,1:T(8,128)} %get-tuple-element.444, f32[512,512,8]{1,0,2:T(8,128)} %get-tuple-element.424, f32[512,8]{0,1:T(8,128)S(1)} %bitcast.90, pred[512,512]{0,1:T(8,128)(4,1)S(1)} %compare_and_fusion.2, f32[512,8]{0,1:T(8,128)S(1)} %get-tuple-element.425, ...), kind=kOutput, calls=%fused_computation.9.clone.1 | convolution fusion | flops 548929536 | bytes 13008901 | tf_op jit(solution)/shard_map/while/body/eval_jaxpr/rkgn,nkd->rkgd/dot_general | solution.py:57
  241.6 29.8 %fusion.23 = bf16[8192,512]{0,1:T(8,128)(2,1)} fusion(bf16[512,1024]{0,1:T(8,128)(2,1)S(1)} %bitcast.94, bf16[8192,1024]{1,0:T(8,128)(2,1)} %param.11), kind=kOutput, calls=%fused_computation.33 | convolution fusion | flops 8594128896 | bytes 26214400 | tf_op jit(solution)/shard_map/dot_general | solution.py:72
  271.5 167.6 %reduce-scatter.2.cloned.1.call-done = bf16[1024,512]{0,1:T(8,128)(2,1)} async-done(((bf16[8192,512]{0,1:T(8,128)(2,1)}), bf16[1024,512]{0,1:T(8,128)(2,1)}) %reduce-scatter.2.cloned.1.call-update) | async-done | bytes 1048592 | tf_op jit(solution)/shard_map/reduce_scatter | solution.py:71
  439.0 2.3 copy.32
  (129 shorter events, 31.3 us)
Async XLA Ops:
  6.5 4.3 copy-start
  6.5 54.3 %all-gather.5.cloned.1.call-start = ((), (), s32[]{:S(2)}) async-start(), calls=%async_computation.3 | async-start | bytes 1114112 | tf_op jit(solution)/shard_map/all_gather | solution.py:29
  8.2 100.0 %all-gather.3.cloned.1.call-start = ((), (), s32[]{:S(2)}) async-start(), calls=%async_computation.2 | async-start | bytes 1114112 | tf_op jit(solution)/shard_map/all_gather | solution.py:28
  13.0 27.4 %all-to-all-start = ((bf16[16,32,1024]{2,1,0:T(8,128)(2,1)}), bf16[16,32,1024]{2,1,0:T(8,128)(2,1)S(1)}, u32[]{:S(2)}, u32[]{:S(2)}) async-start(bf16[16,32,1024]{2,1,0:T(8,128)(2,1)} %copy.29), calls=%async_computation | async-start | bytes 2097152 | tf_op jit(solution)/shard_map/all_to_all | solution.py:96
  22.5 416.6 %reduce-scatter.2.cloned.1.call-start = ((), (), s32[]{:S(2)}) async-start(), calls=%async_computation.4 | async-start | bytes 9437184 | tf_op jit(solution)/shard_map/reduce_scatter | solution.py:71
  114.4 7.7 %copy-start.1 = (f32[512,512,8]{1,0,2:T(8,128)S(1)}, f32[512,512,8]{1,0,2:T(8,128)}, u32[]{:S(2)}) copy-start(f32[512,512,8]{1,0,2:T(8,128)} %get-tuple-element.424) | copy-start | bytes 25165828 | tf_op jit(solution)/shard_map/while
  130.3 8.3 %copy-start.1 = (f32[512,512,8]{1,0,2:T(8,128)S(1)}, f32[512,512,8]{1,0,2:T(8,128)}, u32[]{:S(2)}) copy-start(f32[512,512,8]{1,0,2:T(8,128)} %get-tuple-element.424) | copy-start | bytes 25165828 | tf_op jit(solution)/shard_map/while
  146.8 8.3 %copy-start.1 = (f32[512,512,8]{1,0,2:T(8,128)S(1)}, f32[512,512,8]{1,0,2:T(8,128)}, u32[]{:S(2)}) copy-start(f32[512,512,8]{1,0,2:T(8,128)} %get-tuple-element.424) | copy-start | bytes 25165828 | tf_op jit(solution)/shard_map/while
  163.3 8.3 %copy-start.1 = (f32[512,512,8]{1,0,2:T(8,128)S(1)}, f32[512,512,8]{1,0,2:T(8,128)}, u32[]{:S(2)}) copy-start(f32[512,512,8]{1,0,2:T(8,128)} %get-tuple-element.424) | copy-start | bytes 25165828 | tf_op jit(solution)/shard_map/while
  179.8 8.3 %copy-start.1 = (f32[512,512,8]{1,0,2:T(8,128)S(1)}, f32[512,512,8]{1,0,2:T(8,128)}, u32[]{:S(2)}) copy-start(f32[512,512,8]{1,0,2:T(8,128)} %get-tuple-element.424) | copy-start | bytes 25165828 | tf_op jit(solution)/shard_map/while
  196.4 8.3 %copy-start.1 = (f32[512,512,8]{1,0,2:T(8,128)S(1)}, f32[512,512,8]{1,0,2:T(8,128)}, u32[]{:S(2)}) copy-start(f32[512,512,8]{1,0,2:T(8,128)} %get-tuple-element.424) | copy-start | bytes 25165828 | tf_op jit(solution)/shard_map/while
  212.9 8.3 %copy-start.1 = (f32[512,512,8]{1,0,2:T(8,128)S(1)}, f32[512,512,8]{1,0,2:T(8,128)}, u32[]{:S(2)}) copy-start(f32[512,512,8]{1,0,2:T(8,128)} %get-tuple-element.424) | copy-start | bytes 25165828 | tf_op jit(solution)/shard_map/while
  229.4 8.3 %copy-start.1 = (f32[512,512,8]{1,0,2:T(8,128)S(1)}, f32[512,512,8]{1,0,2:T(8,128)}, u32[]{:S(2)}) copy-start(f32[512,512,8]{1,0,2:T(8,128)} %get-tuple-element.424) | copy-start | bytes 25165828 | tf_op jit(solution)/shard_map/while
Sparse Core Ops, SparseCore 0:
  9.6 51.1 all-gather.4
  63.3 44.8 all-gather.2
  271.6 167.4 reduce-scatter.1
where the time goes:
time: 448 us
  waiting for transfers between devices  252 us (56%)
  matrix products  141 us (31%)
  other arithmetic  24.2 us (5%)
  between operations  13.2 us (3%)
  starting transfers between devices  9.54 us (2%)
  local copies, waits for them, and re-layouts  7.97 us (2%)
    reduce_scatter x1, waiting for transfers between devices, project(): lax.psum_scatter(lax.dot_general(out_weight, context, (((1,), (1,)), ((),...  168 us
    dot_general x8, matrix products, one_tile(): jnp.einsum('rkgn,nkd->rkgd', weights.astype(jnp.bfloat16), value_block, p...  65.4 us
    all_gather x1, waiting for transfers between devices, attend(): key_piece = lax.all_gather(keys, 'ctx', axis=0, tiled=True)  47.4 us
    dot_general x8, matrix products, one_tile(): jnp.einsum('rkgd,nkd->rkgn', query_heads, key_block, preferred_element_ty...  44.9 us
    dot_general x1, matrix products, project(): lax.dot_general(out_weight, context, (((1,), (1,)), ((), ())), preferred_...  29.8 us
    all_gather x1, waiting for transfers between devices, attend(): value_piece = lax.all_gather(values, 'ctx', axis=0, tiled=True)  20.1 us
    reduce_sum x8, other arithmetic, one_tile(): new_sum = running_sum * factor + jnp.sum(weights, axis=-1)  16.1 us
    all_to_all x1, waiting for transfers between devices, per_device(): lax.all_to_all(outgoing, 'ctx', split_axis=0, concat_axis=0, tiled=True)  15.9 us
  transfers between devices with their start and end apart: 4, of which 4 were waited for; matrix products, arithmetic and copies ran while one was open for 1% of the time, Pallas kernels for 0%

commit v1 on v0

--- a/solution.py
+++ b/solution.py
@@ -26,7 +26,10 @@
         jnp.zeros((row_count, key_heads, group_length, HEAD_SIZE), jnp.float32),
     )
     key_piece = lax.all_gather(keys, "ctx", axis=0, tiled=True)
-    value_piece = lax.all_gather(values, "ctx", axis=0, tiled=True)
+    group_core = lambda page: jnp.concatenate(
+        lax.all_to_all(jnp.stack([page for _ in range(lax.axis_size("ctx"))], 0), "ctx", 0, 0), 0
+    )
+    value_piece = group_core(values)
     piece_rows = key_piece.shape[0]
     tile_rows = math.gcd(piece_rows, 512)
 

time: 448 us -> 410 us (0.915)
  waiting for transfers between devices: 252 us -> 209 us
    all_gather x1, waiting for transfers between devices: 47.4 us -> 8.56 us  [attend(): key_piece = lax.all_gather(keys, 'ctx', axis=0, tiled=True)]
    all_gather x1 -> x0, waiting for transfers between devices: 20.1 us -> none  [attend(): value_piece = lax.all_gather(values, 'ctx', axis=0, tiled=True)]
    all_to_all x0 -> x1, waiting for transfers between devices: none -> 16.3 us  [attend(): lax.all_to_all(jnp.stack([page for _ in range(lax.axis_size('ctx'))], 0),...]
where the time goes in v1:
time: 410 us; the launch traced here: 409 us
  waiting for transfers between devices  209 us (51%)
  matrix products  140 us (34%)
  other arithmetic  23.6 us (6%)
  starting transfers between devices  13.9 us (3%)
  between operations  13.5 us (3%)
  local copies, waits for them, and re-layouts  9.02 us (2%)
    reduce_scatter x1, waiting for transfers between devices, project(): lax.psum_scatter(lax.dot_general(out_weight, context, (((1,), (1,)), ((),...  168 us
    dot_general x8, matrix products, one_tile(): jnp.einsum('rkgn,nkd->rkgd', weights.astype(jnp.bfloat16), value_block, p...  64.8 us
    dot_general x8, matrix products, one_tile(): jnp.einsum('rkgd,nkd->rkgn', query_heads, key_block, preferred_element_ty...  44.9 us
    dot_general x1, matrix products, project(): lax.dot_general(out_weight, context, (((1,), (1,)), ((), ())), preferred_...  29.8 us
    all_to_all x1, waiting for transfers between devices, attend(): lax.all_to_all(jnp.stack([page for _ in range(lax.axis_size('ctx'))], 0),...  16.3 us
    reduce_sum x8, other arithmetic, one_tile(): new_sum = running_sum * factor + jnp.sum(weights, axis=-1)  16.1 us
    all_to_all x1, waiting for transfers between devices, per_device(): lax.all_to_all(outgoing, 'ctx', split_axis=0, concat_axis=0, tiled=True)  15.4 us
    all_to_all x1, starting transfers between devices, per_device(): lax.all_to_all(outgoing, 'ctx', split_axis=0, concat_axis=0, tiled=True)  9.46 us
  transfers between devices with their start and end apart: 4, of which 4 were waited for; matrix products, arithmetic and copies ran while one was open for 1% of the time, Pallas kernels for 0%

profile of v1, /device:TPU:1, one launch (start us, length us, event | category | flops | bytes accessed | tf_op | source)
XLA Modules:
  0.0 409.3 jit_solution(2171669119722088840)
XLA Ops:
  10.6 9.5 %all-to-all-start = ((bf16[16,32,1024]{2,1,0:T(8,128)(2,1)}), bf16[16,32,1024]{2,1,0:T(8,128)(2,1)S(1)}, u32[]{:S(2)}, u32[]{:S(2)}) async-start(bf16[16,32,1024]{2,1,0:T(8,128)(2,1)} %copy.38), calls=%async_computation | async-start | bytes 2097152 | tf_op jit(solution)/shard_map/all_to_all | solution.py:99
  21.9 15.4 %all-to-all-done = bf16[16,32,1024]{2,1,0:T(8,128)(2,1)S(1)} async-done(((bf16[16,32,1024]{2,1,0:T(8,128)(2,1)}), bf16[16,32,1024]{2,1,0:T(8,128)(2,1)S(1)}, u32[]{:S(2)}, u32[]{:S(2)}) %all-to-all-start) | async-done | bytes 1048608 | tf_op jit(solution)/shard_map/all_to_all | solution.py:99
  38.3 4.4 %all-to-all-start.1 = ((bf16[16,256,128]{1,2,0:T(8,128)(2,1)}), bf16[16,256,128]{1,2,0:T(8,128)(2,1)S(1)}, u32[]{:S(2)}, u32[]{:S(2)}) async-start(bf16[16,256,128]{1,2,0:T(8,128)(2,1)} %stack.2), calls=%async_computation.1 | async-start | bytes 2097152 | tf_op jit(solution)/shard_map/all_to_all | solution.py:30
  43.7 16.3 %all-to-all-done.1 = bf16[16,256,128]{1,2,0:T(8,128)(2,1)S(1)} async-done(((bf16[16,256,128]{1,2,0:T(8,128)(2,1)}), bf16[16,256,128]{1,2,0:T(8,128)(2,1)S(1)}, u32[]{:S(2)}, u32[]{:S(2)}) %all-to-all-start.1) | async-done | bytes 1048608 | tf_op jit(solution)/shard_map/all_to_all | solution.py:30
  61.3 8.6 %all-gather.2.cloned.1.call-done = bf16[4096,128]{1,0:T(8,128)(2,1)} async-done(((bf16[256,128]{1,0:T(8,128)(2,1)}), bf16[4096,128]{1,0:T(8,128)(2,1)}) %all-gather.2.cloned.1.call-update) | async-done | bytes 1048592 | tf_op jit(solution)/shard_map/all_gather | solution.py:28
  69.9 130.9 %while.20 = (s32[]{:T(128)}, f32[512,1,8]{0,2,1:T(8,128)S(1)}, f32[512,1,8]{0,2,1:T(8,128)S(1)}, f32[512,1,8,128]{0,3,2,1:T(8,128)}, s32[512]{0:T(512)S(1)}, /*i...) while((s32[]{:T(128)}, f32[512,1,8]{0,2,1:T(8,128)S(1)}, ...), condition=%wide.region_8.9_spmd.clone, body=%wide.region_4.8_spmd.clone.sunk | while | flops 1103414784 | bytes 65560956 | solution.py:68
  70.4 5.6 %fusion.37 = (f32[512,8]{0,1:T(8,128)S(1)}, f32[512,512,8]{1,0,2:T(8,128)}) fusion(pred[512,512]{0,1:T(8,128)(4,1)S(1)} %compare_and_fusion.2, bf16[512,1,8,128]{3,0,2,1:T(8,128)(2,1)S(1)} %get-tuple-element.474, bf16[4096,128]{1,0:T(8,128)(2,1)} %get-tuple-element.473, s32[]{:T(128)S(6)} %select_n.96), kind=kOutput, calls=%fused_computation.3.clone.1 | convolution fusion | flops 543158272 | bytes 9846788 | tf_op jit(solution)/shard_map/while/body/eval_jaxpr/rkgd,nkd->rkgn/dot_general | solution.py:51
  76.0 7.6 %bitcast_add_fusion.5 = f32[512,1,8,128]{0,3,2,1:T(8,128)} fusion(f32[512,1,8,128]{0,3,2,1:T(8,128)} %get-tuple-element.455, f32[512,512,8]{1,0,2:T(8,128)} %get-tuple-element.435, f32[512,8]{0,1:T(8,128)S(1)} %bitcast.92, pred[512,512]{0,1:T(8,128)(4,1)S(1)} %compare_and_fusion.2, f32[512,8]{0,1:T(8,128)S(1)} %get-tuple-element.436, ...), kind=kOutput, calls=%fused_computation.9.clone.1 | convolution fusion | flops 548929536 | bytes 13008901 | tf_op jit(solution)/shard_map/while/body/eval_jaxpr/rkgn,nkd->rkgd/dot_general | solution.py:60
  86.3 5.6 %fusion.37 = (f32[512,8]{0,1:T(8,128)S(1)}, f32[512,512,8]{1,0,2:T(8,128)}) fusion(pred[512,512]{0,1:T(8,128)(4,1)S(1)} %compare_and_fusion.2, bf16[512,1,8,128]{3,0,2,1:T(8,128)(2,1)S(1)} %get-tuple-element.474, bf16[4096,128]{1,0:T(8,128)(2,1)} %get-tuple-element.473, s32[]{:T(128)S(6)} %select_n.96), kind=kOutput, calls=%fused_computation.3.clone.1 | convolution fusion | flops 543158272 | bytes 9846788 | tf_op jit(solution)/shard_map/while/body/eval_jaxpr/rkgd,nkd->rkgn/dot_general | solution.py:51
  91.9 8.2 %bitcast_add_fusion.5 = f32[512,1,8,128]{0,3,2,1:T(8,128)} fusion(f32[512,1,8,128]{0,3,2,1:T(8,128)} %get-tuple-element.455, f32[512,512,8]{1,0,2:T(8,128)} %get-tuple-element.435, f32[512,8]{0,1:T(8,128)S(1)} %bitcast.92, pred[512,512]{0,1:T(8,128)(4,1)S(1)} %compare_and_fusion.2, f32[512,8]{0,1:T(8,128)S(1)} %get-tuple-element.436, ...), kind=kOutput, calls=%fused_computation.9.clone.1 | convolution fusion | flops 548929536 | bytes 13008901 | tf_op jit(solution)/shard_map/while/body/eval_jaxpr/rkgn,nkd->rkgd/dot_general | solution.py:60
  102.7 5.6 %fusion.37 = (f32[512,8]{0,1:T(8,128)S(1)}, f32[512,512,8]{1,0,2:T(8,128)}) fusion(pred[512,512]{0,1:T(8,128)(4,1)S(1)} %compare_and_fusion.2, bf16[512,1,8,128]{3,0,2,1:T(8,128)(2,1)S(1)} %get-tuple-element.474, bf16[4096,128]{1,0:T(8,128)(2,1)} %get-tuple-element.473, s32[]{:T(128)S(6)} %select_n.96), kind=kOutput, calls=%fused_computation.3.clone.1 | convolution fusion | flops 543158272 | bytes 9846788 | tf_op jit(solution)/shard_map/while/body/eval_jaxpr/rkgd,nkd->rkgn/dot_general | solution.py:51
  108.3 8.2 %bitcast_add_fusion.5 = f32[512,1,8,128]{0,3,2,1:T(8,128)} fusion(f32[512,1,8,128]{0,3,2,1:T(8,128)} %get-tuple-element.455, f32[512,512,8]{1,0,2:T(8,128)} %get-tuple-element.435, f32[512,8]{0,1:T(8,128)S(1)} %bitcast.92, pred[512,512]{0,1:T(8,128)(4,1)S(1)} %compare_and_fusion.2, f32[512,8]{0,1:T(8,128)S(1)} %get-tuple-element.436, ...), kind=kOutput, calls=%fused_computation.9.clone.1 | convolution fusion | flops 548929536 | bytes 13008901 | tf_op jit(solution)/shard_map/while/body/eval_jaxpr/rkgn,nkd->rkgd/dot_general | solution.py:60
  119.1 5.6 %fusion.37 = (f32[512,8]{0,1:T(8,128)S(1)}, f32[512,512,8]{1,0,2:T(8,128)}) fusion(pred[512,512]{0,1:T(8,128)(4,1)S(1)} %compare_and_fusion.2, bf16[512,1,8,128]{3,0,2,1:T(8,128)(2,1)S(1)} %get-tuple-element.474, bf16[4096,128]{1,0:T(8,128)(2,1)} %get-tuple-element.473, s32[]{:T(128)S(6)} %select_n.96), kind=kOutput, calls=%fused_computation.3.clone.1 | convolution fusion | flops 543158272 | bytes 9846788 | tf_op jit(solution)/shard_map/while/body/eval_jaxpr/rkgd,nkd->rkgn/dot_general | solution.py:51
  124.8 8.2 %bitcast_add_fusion.5 = f32[512,1,8,128]{0,3,2,1:T(8,128)} fusion(f32[512,1,8,128]{0,3,2,1:T(8,128)} %get-tuple-element.455, f32[512,512,8]{1,0,2:T(8,128)} %get-tuple-element.435, f32[512,8]{0,1:T(8,128)S(1)} %bitcast.92, pred[512,512]{0,1:T(8,128)(4,1)S(1)} %compare_and_fusion.2, f32[512,8]{0,1:T(8,128)S(1)} %get-tuple-element.436, ...), kind=kOutput, calls=%fused_computation.9.clone.1 | convolution fusion | flops 548929536 | bytes 13008901 | tf_op jit(solution)/shard_map/while/body/eval_jaxpr/rkgn,nkd->rkgd/dot_general | solution.py:60
  135.6 5.6 %fusion.37 = (f32[512,8]{0,1:T(8,128)S(1)}, f32[512,512,8]{1,0,2:T(8,128)}) fusion(pred[512,512]{0,1:T(8,128)(4,1)S(1)} %compare_and_fusion.2, bf16[512,1,8,128]{3,0,2,1:T(8,128)(2,1)S(1)} %get-tuple-element.474, bf16[4096,128]{1,0:T(8,128)(2,1)} %get-tuple-element.473, s32[]{:T(128)S(6)} %select_n.96), kind=kOutput, calls=%fused_computation.3.clone.1 | convolution fusion | flops 543158272 | bytes 9846788 | tf_op jit(solution)/shard_map/while/body/eval_jaxpr/rkgd,nkd->rkgn/dot_general | solution.py:51
  141.2 8.2 %bitcast_add_fusion.5 = f32[512,1,8,128]{0,3,2,1:T(8,128)} fusion(f32[512,1,8,128]{0,3,2,1:T(8,128)} %get-tuple-element.455, f32[512,512,8]{1,0,2:T(8,128)} %get-tuple-element.435, f32[512,8]{0,1:T(8,128)S(1)} %bitcast.92, pred[512,512]{0,1:T(8,128)(4,1)S(1)} %compare_and_fusion.2, f32[512,8]{0,1:T(8,128)S(1)} %get-tuple-element.436, ...), kind=kOutput, calls=%fused_computation.9.clone.1 | convolution fusion | flops 548929536 | bytes 13008901 | tf_op jit(solution)/shard_map/while/body/eval_jaxpr/rkgn,nkd->rkgd/dot_general | solution.py:60
  152.0 5.6 %fusion.37 = (f32[512,8]{0,1:T(8,128)S(1)}, f32[512,512,8]{1,0,2:T(8,128)}) fusion(pred[512,512]{0,1:T(8,128)(4,1)S(1)} %compare_and_fusion.2, bf16[512,1,8,128]{3,0,2,1:T(8,128)(2,1)S(1)} %get-tuple-element.474, bf16[4096,128]{1,0:T(8,128)(2,1)} %get-tuple-element.473, s32[]{:T(128)S(6)} %select_n.96), kind=kOutput, calls=%fused_computation.3.clone.1 | convolution fusion | flops 543158272 | bytes 9846788 | tf_op jit(solution)/shard_map/while/body/eval_jaxpr/rkgd,nkd->rkgn/dot_general | solution.py:51
  157.6 8.2 %bitcast_add_fusion.5 = f32[512,1,8,128]{0,3,2,1:T(8,128)} fusion(f32[512,1,8,128]{0,3,2,1:T(8,128)} %get-tuple-element.455, f32[512,512,8]{1,0,2:T(8,128)} %get-tuple-element.435, f32[512,8]{0,1:T(8,128)S(1)} %bitcast.92, pred[512,512]{0,1:T(8,128)(4,1)S(1)} %compare_and_fusion.2, f32[512,8]{0,1:T(8,128)S(1)} %get-tuple-element.436, ...), kind=kOutput, calls=%fused_computation.9.clone.1 | convolution fusion | flops 548929536 | bytes 13008901 | tf_op jit(solution)/shard_map/while/body/eval_jaxpr/rkgn,nkd->rkgd/dot_general | solution.py:60
  168.4 5.6 %fusion.37 = (f32[512,8]{0,1:T(8,128)S(1)}, f32[512,512,8]{1,0,2:T(8,128)}) fusion(pred[512,512]{0,1:T(8,128)(4,1)S(1)} %compare_and_fusion.2, bf16[512,1,8,128]{3,0,2,1:T(8,128)(2,1)S(1)} %get-tuple-element.474, bf16[4096,128]{1,0:T(8,128)(2,1)} %get-tuple-element.473, s32[]{:T(128)S(6)} %select_n.96), kind=kOutput, calls=%fused_computation.3.clone.1 | convolution fusion | flops 543158272 | bytes 9846788 | tf_op jit(solution)/shard_map/while/body/eval_jaxpr/rkgd,nkd->rkgn/dot_general | solution.py:51
  174.1 8.2 %bitcast_add_fusion.5 = f32[512,1,8,128]{0,3,2,1:T(8,128)} fusion(f32[512,1,8,128]{0,3,2,1:T(8,128)} %get-tuple-element.455, f32[512,512,8]{1,0,2:T(8,128)} %get-tuple-element.435, f32[512,8]{0,1:T(8,128)S(1)} %bitcast.92, pred[512,512]{0,1:T(8,128)(4,1)S(1)} %compare_and_fusion.2, f32[512,8]{0,1:T(8,128)S(1)} %get-tuple-element.436, ...), kind=kOutput, calls=%fused_computation.9.clone.1 | convolution fusion | flops 548929536 | bytes 13008901 | tf_op jit(solution)/shard_map/while/body/eval_jaxpr/rkgn,nkd->rkgd/dot_general | solution.py:60
  184.9 5.6 %fusion.37 = (f32[512,8]{0,1:T(8,128)S(1)}, f32[512,512,8]{1,0,2:T(8,128)}) fusion(pred[512,512]{0,1:T(8,128)(4,1)S(1)} %compare_and_fusion.2, bf16[512,1,8,128]{3,0,2,1:T(8,128)(2,1)S(1)} %get-tuple-element.474, bf16[4096,128]{1,0:T(8,128)(2,1)} %get-tuple-element.473, s32[]{:T(128)S(6)} %select_n.96), kind=kOutput, calls=%fused_computation.3.clone.1 | convolution fusion | flops 543158272 | bytes 9846788 | tf_op jit(solution)/shard_map/while/body/eval_jaxpr/rkgd,nkd->rkgn/dot_general | solution.py:51
  190.5 8.2 %bitcast_add_fusion.5 = f32[512,1,8,128]{0,3,2,1:T(8,128)} fusion(f32[512,1,8,128]{0,3,2,1:T(8,128)} %get-tuple-element.455, f32[512,512,8]{1,0,2:T(8,128)} %get-tuple-element.435, f32[512,8]{0,1:T(8,128)S(1)} %bitcast.92, pred[512,512]{0,1:T(8,128)(4,1)S(1)} %compare_and_fusion.2, f32[512,8]{0,1:T(8,128)S(1)} %get-tuple-element.436, ...), kind=kOutput, calls=%fused_computation.9.clone.1 | convolution fusion | flops 548929536 | bytes 13008901 | tf_op jit(solution)/shard_map/while/body/eval_jaxpr/rkgn,nkd->rkgd/dot_general | solution.py:60
  202.6 29.8 %fusion.23 = bf16[8192,512]{0,1:T(8,128)(2,1)} fusion(bf16[512,1024]{0,1:T(8,128)(2,1)S(1)} %bitcast.96, bf16[8192,1024]{1,0:T(8,128)(2,1)} %param.11), kind=kOutput, calls=%fused_computation.33 | convolution fusion | flops 8594128896 | bytes 26214400 | tf_op jit(solution)/shard_map/dot_general | solution.py:75
  232.5 167.7 %reduce-scatter.2.cloned.1.call-done = bf16[1024,512]{0,1:T(8,128)(2,1)} async-done(((bf16[8192,512]{0,1:T(8,128)(2,1)}), bf16[1024,512]{0,1:T(8,128)(2,1)}) %reduce-scatter.2.cloned.1.call-update) | async-done | bytes 1048592 | tf_op jit(solution)/shard_map/reduce_scatter | solution.py:74
  (132 shorter events, 33.9 us)
Async XLA Ops:
  6.5 1.9 copy-start
  6.5 36.4 %copy-start.2 = (s32[16]{0:T(128)S(1)}, s32[16]{0:T(128)}, u32[]{:S(2)}) copy-start(s32[16]{0:T(128)} %param.12) | copy-start | bytes 196
  10.6 26.7 %all-to-all-start = ((bf16[16,32,1024]{2,1,0:T(8,128)(2,1)}), bf16[16,32,1024]{2,1,0:T(8,128)(2,1)S(1)}, u32[]{:S(2)}, u32[]{:S(2)}) async-start(bf16[16,32,1024]{2,1,0:T(8,128)(2,1)} %copy.38), calls=%async_computation | async-start | bytes 2097152 | tf_op jit(solution)/shard_map/all_to_all | solution.py:99
  20.1 49.8 %all-gather.2.cloned.1.call-start = ((), (), s32[]{:S(2)}) async-start(), calls=%async_computation.3 | async-start | bytes 1114112 | tf_op jit(solution)/shard_map/all_gather | solution.py:28
  38.3 21.6 %all-to-all-start.1 = ((bf16[16,256,128]{1,2,0:T(8,128)(2,1)}), bf16[16,256,128]{1,2,0:T(8,128)(2,1)S(1)}, u32[]{:S(2)}, u32[]{:S(2)}) async-start(bf16[16,256,128]{1,2,0:T(8,128)(2,1)} %stack.2), calls=%async_computation.1 | async-start | bytes 2097152 | tf_op jit(solution)/shard_map/all_to_all | solution.py:30
  42.7 357.4 %reduce-scatter.2.cloned.1.call-start = ((), (), s32[]{:S(2)}) async-start(), calls=%async_computation.4 | async-start | bytes 9437184 | tf_op jit(solution)/shard_map/reduce_scatter | solution.py:74
  76.0 7.6 %copy-start.1 = (f32[512,512,8]{1,0,2:T(8,128)S(1)}, f32[512,512,8]{1,0,2:T(8,128)}, u32[]{:S(2)}) copy-start(f32[512,512,8]{1,0,2:T(8,128)} %get-tuple-element.435) | copy-start | bytes 25165828 | tf_op jit(solution)/shard_map/while
  91.9 8.2 %copy-start.1 = (f32[512,512,8]{1,0,2:T(8,128)S(1)}, f32[512,512,8]{1,0,2:T(8,128)}, u32[]{:S(2)}) copy-start(f32[512,512,8]{1,0,2:T(8,128)} %get-tuple-element.435) | copy-start | bytes 25165828 | tf_op jit(solution)/shard_map/while
  108.3 8.2 %copy-start.1 = (f32[512,512,8]{1,0,2:T(8,128)S(1)}, f32[512,512,8]{1,0,2:T(8,128)}, u32[]{:S(2)}) copy-start(f32[512,512,8]{1,0,2:T(8,128)} %get-tuple-element.435) | copy-start | bytes 25165828 | tf_op jit(solution)/shard_map/while
  124.8 8.2 %copy-start.1 = (f32[512,512,8]{1,0,2:T(8,128)S(1)}, f32[512,512,8]{1,0,2:T(8,128)}, u32[]{:S(2)}) copy-start(f32[512,512,8]{1,0,2:T(8,128)} %get-tuple-element.435) | copy-start | bytes 25165828 | tf_op jit(solution)/shard_map/while
  141.2 8.2 %copy-start.1 = (f32[512,512,8]{1,0,2:T(8,128)S(1)}, f32[512,512,8]{1,0,2:T(8,128)}, u32[]{:S(2)}) copy-start(f32[512,512,8]{1,0,2:T(8,128)} %get-tuple-element.435) | copy-start | bytes 25165828 | tf_op jit(solution)/shard_map/while
  157.6 8.2 %copy-start.1 = (f32[512,512,8]{1,0,2:T(8,128)S(1)}, f32[512,512,8]{1,0,2:T(8,128)}, u32[]{:S(2)}) copy-start(f32[512,512,8]{1,0,2:T(8,128)} %get-tuple-element.435) | copy-start | bytes 25165828 | tf_op jit(solution)/shard_map/while
  174.1 8.2 %copy-start.1 = (f32[512,512,8]{1,0,2:T(8,128)S(1)}, f32[512,512,8]{1,0,2:T(8,128)}, u32[]{:S(2)}) copy-start(f32[512,512,8]{1,0,2:T(8,128)} %get-tuple-element.435) | copy-start | bytes 25165828 | tf_op jit(solution)/shard_map/while
  190.5 8.2 %copy-start.1 = (f32[512,512,8]{1,0,2:T(8,128)S(1)}, f32[512,512,8]{1,0,2:T(8,128)}, u32[]{:S(2)}) copy-start(f32[512,512,8]{1,0,2:T(8,128)} %get-tuple-element.435) | copy-start | bytes 25165828 | tf_op jit(solution)/shard_map/while
Sparse Core Ops, SparseCore 0:
  23.4 46.4 all-gather.1
  232.6 167.4 reduce-scatter.1
